TPU v7x, 256 devices: a whole 4x4x8 slice. The times are simulated.
256 devices in a mesh: ga: 16 (over z_lo, y), pair: 16 (over z_hi, x, core).
Axes of the slice: x: 4, y: 4, z: 8 (z_hi: 2, z_lo: 4; z = z_hi * 4 + z_lo), core: 2. Of those that a mesh axis runs over, the one named last changes fastest.
Arguments:
- val_density: bfloat16 [256, 3, 2, 8192], P('pair', None, None, 'ga'), may hold values from -0.0625 to 0.0625
- con_density: bfloat16 [576, 3, 2, 8192], P('ga', None, None, 'pair'), may hold values from -6 to 6
- screened: bfloat16 [3, 2, 8192, 8192], P(None, None, 'ga', 'pair'), may hold values from -0.0625 to 0.0625
- coulomb: float32 [3, 8192], P(None, 'ga'), may hold values from 0.2 to 2
- trans_here: bfloat16 [384, 2, 8192], P('pair', None, 'ga'), may hold values from -6 to 6
- trans_there: bfloat16 [384, 3, 2, 8192], P('pair', None, None, 'ga'), may hold values from -0.0625 to 0.0625
- shift_map: int32 [3, 8192], P(None, 'pair'), may hold values from 0 to 8191, as said below
- ordering: int32 [384], replicated, may hold values from 0 to 383, each once
Outputs:
- kernel: float32 [3, 2, 384, 384], P(None, None, 'pair', 'ga')
Inputs may be any that keep to these rules, and one draw needn't show every extreme that they name: `shift_map`: each aligned block of 128 entries of a row is a permutation of that block's own G-vector indices.
All inputs are finite; a program needn't handle non-finite values.
Results may differ from a plain program's by a relative error of at most 0.0003.
Values may be sent and summed in bfloat16 or wider, within the bound.
A program may use at most 64 MiB of HBM per device.

v0:
```python
import jax
import jax.numpy as jnp
from jax import lax
from jax.sharding import PartitionSpec as P

NV = 16
NC = 24
GBLK = 128
NT = 384
F32 = jnp.float32
BF16 = jnp.bfloat16


def two_terms(values):
    high = lax.reduce_precision(values, exponent_bits=8, mantissa_bits=7)
    low = lax.reduce_precision(values - high, exponent_bits=8, mantissa_bits=7)
    return (high.astype(BF16), low.astype(BF16))


def on_device(
    val_density, con_density, screened, coulomb, trans_here, trans_there, shift_map, ordering
):
    con_count, points, _, slab_cols = con_density.shape
    blocks = slab_cols // GBLK
    pairs = lax.axis_size("pair")
    slabs = lax.axis_size("ga")
    whole_con = lax.all_gather(con_density, "ga", axis=0, tiled=True)
    whole_val = lax.all_gather(val_density, "pair", axis=0, tiled=True)
    whole_here = lax.all_gather(trans_here, "pair", axis=0, tiled=True)
    within = (shift_map % GBLK).reshape(points, blocks, GBLK)
    onehot = (
        within[:, :, :, None] == jnp.arange(GBLK, dtype=jnp.int32)[None, None, None, :]
    ).astype(BF16)

    def mul(spec, left, right):
        return jnp.einsum(spec, left, right, preferred_element_type=F32)

    rows_re = mul("akg,kgh->kah", whole_val[:, :, 0], screened[:, 0]) - mul(
        "akg,kgh->kah", whole_val[:, :, 1], screened[:, 1]
    )
    rows_im = mul("akg,kgh->kah", whole_val[:, :, 0], screened[:, 1]) + mul(
        "akg,kgh->kah", whole_val[:, :, 1], screened[:, 0]
    )
    shape = (points, NV * NV, blocks, GBLK)

    def unshift(term):
        moved = mul("kang,kngh->kanh", term.reshape(shape), onehot).astype(BF16)
        return moved.reshape(points, NV * NV, slab_cols)

    real = [unshift(term) for term in two_terms(rows_re)]
    imag = [unshift(term) for term in two_terms(rows_im)]
    left_re = jnp.concatenate([real[0], -imag[0], real[1], -imag[1]], axis=2)
    left_im = jnp.concatenate([imag[0], real[0], imag[1], real[1]], axis=2)
    con_rows = jnp.transpose(whole_con, (1, 0, 2, 3)).reshape(points, NC * NC, 2 * slab_cols)
    con_twice = jnp.concatenate([con_rows, con_rows], axis=2)
    direct = jnp.stack(
        [mul("kax,kbx->kab", left_re, con_twice), mul("kax,kbx->kab", left_im, con_twice)], axis=1
    )
    direct = jnp.transpose(direct.reshape(points, 2, NV, NV, NC * NC), (3, 0, 1, 2, 4))
    direct = lax.psum_scatter(direct, "pair", scatter_dimension=0, tiled=True)[0]
    direct = jnp.transpose(direct.reshape(points, 2, NV, NC, NC), (2, 3, 0, 1, 4)).reshape(
        NT, points, 2, NC
    )
    weighted = trans_there.astype(F32) * coulomb[None, :, None, :]
    high = lax.Precision.HIGHEST
    here = whole_here.astype(F32)
    exch_re = jnp.einsum("tg,skg->tks", here[:, 0], weighted[:, :, 0], precision=high) - jnp.einsum(
        "tg,skg->tks", here[:, 1], weighted[:, :, 1], precision=high
    )
    exch_im = jnp.einsum("tg,skg->tks", here[:, 0], weighted[:, :, 1], precision=high) + jnp.einsum(
        "tg,skg->tks", here[:, 1], weighted[:, :, 0], precision=high
    )
    natural = 2.0 * jnp.stack([exch_re, exch_im], axis=2) - direct
    rows = natural[ordering]
    rows = lax.all_to_all(
        rows.reshape(pairs, NT // pairs, points, 2, NC), "pair", split_axis=0, concat_axis=0
    )
    cols = jnp.transpose(rows, (0, 4, 2, 3, 1)).reshape(NT, points * 2 * (NT // pairs))
    cols = cols[ordering]
    cols = lax.psum_scatter(cols, "ga", scatter_dimension=0, tiled=True)
    cols = cols.reshape(NT // slabs, points, 2, NT // pairs)
    return jnp.transpose(cols, (1, 2, 3, 0))


def solution(mesh):
    in_specs = (
        P("pair", None, None, "ga"),
        P("ga", None, None, "pair"),
        P(None, None, "ga", "pair"),
        P(None, "ga"),
        P("pair", None, "ga"),
        P("pair", None, None, "ga"),
        P(None, "pair"),
        P(),
    )
    out_specs = P(None, None, "pair", "ga")
    return jax.shard_map(
        on_device, mesh=mesh, in_specs=in_specs, out_specs=out_specs, check_vma=False
    )
```

profile of v0, /device:TPU:2, one launch (start us, length us, event | category | flops | bytes accessed | tf_op | source)
XLA Modules:
  0.0 404.5 jit_solution(9876181623509086774)
XLA Ops:
  6.5 1.7 copy.57
  8.3 0.7 all-gather.5.cloned.1.call-update
  9.1 0.7 add_select_fusion
  9.8 62.1 %all-gather.3.cloned.1.call-done = bf16[256,3,2,512]{3,0,1,2:T(8,128)(2,1)} async-done(((bf16[16,3,2,512]{3,0,1,2:T(8,128)(2,1)}), bf16[256,3,2,512]{3,0,1,2:T(8,128)(2,1)}) %all-gather.3.cloned.1.call-update) | async-done | bytes 1572880 | tf_op jit(solution)/shard_map/all_gather | solution.py:28
  71.9 2.2 fusion.22
  74.1 2.7 fusion.42
  76.8 1.3 convolution_convert_fusion.1
  78.1 2.3 copy.67
  80.4 1.9 fusion.20
  82.3 1.5 fusion.43
  83.8 0.4 convolution_convert_fusion
  84.2 0.3 copy.65
  84.5 0.5 copy-done.6
  84.9 0.4 convolution_convert_fusion.3
  85.3 1.2 copy.66
  86.6 0.4 convolution_convert_fusion.2
  87.3 1.1 neg.7
  88.4 1.0 neg.6
  89.4 66.7 %all-gather.5.cloned.1.call-done = bf16[576,3,2,512]{3,2,1,0:T(2,128)(2,1)} async-done(((bf16[36,3,2,512]{3,2,1,0:T(2,128)(2,1)}), bf16[576,3,2,512]{3,2,1,0:T(2,128)(2,1)}) %all-gather.5.cloned.1.call-update) | async-done | bytes 3538960 | tf_op jit(solution)/shard_map/all_gather | solution.py:27
  156.1 6.2 %copy.68 = bf16[3,576,2,512]{3,2,1,0:T(2,128)(2,1)} copy(bf16[3,576,2,512]{3,2,0,1:T(2,128)(2,1)} %bitcast.118) | data formatting | bytes 7077888 | tf_op jit(solution)/shard_map/transpose | solution.py:54
  162.4 7.8 %reshape.54 = bf16[3,576,1024]{2,1,0:T(8,128)(2,1)S(1)} reshape(bf16[3,576,2,512]{3,2,1,0:T(2,128)(2,1)} %copy.68) | data formatting | bytes 7077888 | tf_op jit(solution)/shard_map/reshape | solution.py:54
  170.2 0.5 constant_dynamic-update-slice_fusion.1
  170.7 0.5 constant_dynamic-update-slice_fusion
  171.2 0.6 copy-done.3
  172.1 6.3 %fusion.8 = f32[3,256,576]{2,1,0:T(8,128)S(1)} fusion(bf16[3,576,2048]{2,1,0:T(8,128)(2,1)S(1)} %constant_dynamic-update-slice_fusion, bf16[3,256,512]{2,1,0:T(8,128)(2,1)} %copy.67, bf16[3,256,512]{2,1,0:T(8,128)(2,1)S(1)} %copy-done.3, bf16[3,256,512]{2,1,0:T(8,128)(2,1)} %copy.66, bf16[3,256,512]{2,1,0:T(8,128)(2,1)S(1)} %copy-done.5), kind=kOutput, calls=%fused_computation.11 | convolution fusion | flops 1824522240 | bytes 11993088 | tf_op jit(solution)/shard_map/kax,kbx->kab/dot_general | solution.py:36
  178.5 2.6 fusion
  181.4 3.1 copy.75
  184.5 0.7 copy-done.13
  185.4 26.4 %all_gather.9 = bf16[384,2,512]{2,0,1:T(8,128)(2,1)S(1)} all-gather(bf16[24,2,512]{2,0,1:T(8,128)(2,1)S(1)} %copy.56), channel_id=1, replica_groups=mesh['ga'=16,'pair'=16] {'pair'}, dimensions={0}, use_global_device_ids=true | all-gather | bytes 835584 | tf_op jit(solution)/shard_map/all_gather | solution.py:29
  211.8 0.5 fusion.56
  212.3 0.5 fusion.38
  212.8 0.5 fusion.57
  213.3 0.5 fusion.39
  213.8 70.6 %reduce-scatter.3.cloned.1.call-done = f32[1,3,2,16,576]{4,3,2,1,0:T(8,128)} async-done(((f32[16,3,2,16,576]{4,3,2,1,0:T(8,128)}), f32[1,3,2,16,576]{4,3,2,1,0:T(8,128)}) %reduce-scatter.3.cloned.1.call-update) | async-done | bytes 221200 | tf_op jit(solution)/shard_map/reduce_scatter | solution.py:60
  284.4 1.4 reshape_squeeze.3
  285.8 0.3 copy.84
  286.2 1.1 copy.77
  287.2 3.3 gather_fusion
  290.7 0.9 reshape.80
  291.6 13.5 %all_to_all.5 = f32[16,1,3456]{2,1,0:T(1,128)S(1)} all-to-all(f32[16,1,3456]{2,1,0:T(1,128)S(1)} %reshape.80), channel_id=1, replica_groups=mesh['ga'=16,'pair'=16] {'pair'}, dimensions={0} | all-to-all | bytes 442368 | tf_op jit(solution)/shard_map/all_to_all | solution.py:75
  305.1 0.5 broadcast.25
  305.6 1.2 reduce
  306.7 0.7 reshape.81
  307.6 0.8 copy.85
  308.4 0.7 reshape.79
  309.1 2.2 gather_fusion.1
  311.3 85.2 %reduce-scatter.5.cloned.1.call-done = f32[24,144]{1,0:T(8,128)} async-done(((f32[384,144]{1,0:T(8,128)}), f32[24,144]{1,0:T(8,128)}) %reduce-scatter.5.cloned.1.call-update) | async-done | bytes 13840 | tf_op jit(solution)/shard_map/reduce_scatter | solution.py:80
  396.5 1.5 copy.86
  (46 shorter events, 1.4 us)
Async XLA Ops:
  6.5 67.6 %copy-start = (bf16[3,2,512,512]{3,2,1,0:T(8,128)(2,1)S(1)}, bf16[3,2,512,512]{3,2,1,0:T(8,128)(2,1)}, u32[]{:S(2)}) copy-start(bf16[3,2,512,512]{3,2,1,0:T(8,128)(2,1)} %param.10) | copy-start | bytes 9437188
  6.5 65.3 %all-gather.3.cloned.1.call-start = ((), (), s32[]{:S(2)}) async-start(), calls=%async_computation.3 | async-start | bytes 1671168 | tf_op jit(solution)/shard_map/all_gather | solution.py:28
  8.3 147.9 %all-gather.5.cloned.1.call-start = ((), (), s32[]{:S(2)}) async-start(), calls=%async_computation.4 | async-start | bytes 3760128 | tf_op jit(solution)/shard_map/all_gather | solution.py:27
  9.0 275.4 %reduce-scatter.3.cloned.1.call-start = ((), (), s32[]{:S(2)}) async-start(), calls=%async_computation.5 | async-start | bytes 4177920 | tf_op jit(solution)/shard_map/reduce_scatter | solution.py:60
  80.4 1.9 copy-start.1
  83.8 1.1 copy-start.6
  83.8 2.8 copy-start.7
  84.5 2.7 copy-start.2
  87.2 68.9 %copy-start.4 = (bf16[3,256,512]{2,1,0:T(8,128)(2,1)}, bf16[3,256,512]{2,1,0:T(8,128)(2,1)S(1)}, u32[]{:S(2)}) copy-start(bf16[3,256,512]{2,1,0:T(8,128)(2,1)S(1)} %copy.62) | copy-start | bytes 2359300
  170.7 1.1 copy-start.3
  170.7 1.4 copy-start.5
  172.1 6.4 %copy-start.8 = (bf16[3,256,512]{2,1,0:T(8,128)(2,1)S(1)}, bf16[3,256,512]{2,1,0:T(8,128)(2,1)}, u32[]{:S(2)}) copy-start(bf16[3,256,512]{2,1,0:T(8,128)(2,1)} %copy.67) | copy-start | bytes 2359300
  172.1 6.4 %copy-start.9 = (bf16[3,256,512]{2,1,0:T(8,128)(2,1)S(1)}, bf16[3,256,512]{2,1,0:T(8,128)(2,1)}, u32[]{:S(2)}) copy-start(bf16[3,256,512]{2,1,0:T(8,128)(2,1)} %copy.66) | copy-start | bytes 2359300
  172.1 6.4 %copy-start.10 = (bf16[3,256,512]{2,1,0:T(8,128)(2,1)S(1)}, bf16[3,256,512]{2,1,0:T(8,128)(2,1)}, u32[]{:S(2)}) copy-start(bf16[3,256,512]{2,1,0:T(8,128)(2,1)} %neg.7) | copy-start | bytes 2359300
  172.1 6.4 %copy-start.11 = (bf16[3,256,512]{2,1,0:T(8,128)(2,1)S(1)}, bf16[3,256,512]{2,1,0:T(8,128)(2,1)}, u32[]{:S(2)}) copy-start(bf16[3,256,512]{2,1,0:T(8,128)(2,1)} %neg.6) | copy-start | bytes 2359300
  184.4 0.8 copy-start.13
  184.4 0.8 copy-start.15
  184.4 1.0 copy-start.12
  184.4 1.0 copy-start.14
  184.5 212.1 %reduce-scatter.5.cloned.1.call-start = ((), (), s32[]{:S(2)}) async-start(), calls=%async_computation.6 | async-start | bytes 417792 | tf_op jit(solution)/shard_map/reduce_scatter | solution.py:80
Sparse Core Ops, SparseCore 0:
  10.1 61.7 all-gather.2
  73.7 82.4 all-gather.4
  184.6 99.7 reduce-scatter.2
  311.4 85.0 reduce-scatter.4
where the time goes:
time: 405 us
  waiting for transfers between devices  285 us (70%)
  blocking collectives  39.9 us (10%)
  local copies, waits for them, and re-layouts  39.7 us (10%)
  matrix products  21.6 us (5%)
  between operations  13.5 us (3%)
  other arithmetic  4.33 us (1%)
    reduce_scatter x1, waiting for transfers between devices, on_device(): cols = lax.psum_scatter(cols, 'ga', scatter_dimension=0, tiled=True)  85.2 us
    reduce_scatter x1, waiting for transfers between devices, on_device(): lax.psum_scatter(direct, 'pair', scatter_dimension=0, tiled=True)[0]  70.6 us
    all_gather x1, waiting for transfers between devices, on_device(): whole_con = lax.all_gather(con_density, 'ga', axis=0, tiled=True)  66.7 us
    all_gather x1, waiting for transfers between devices, on_device(): whole_val = lax.all_gather(val_density, 'pair', axis=0, tiled=True)  62.1 us
    all_gather x1, blocking collectives, on_device(): whole_here = lax.all_gather(trans_here, 'pair', axis=0, tiled=True)  26.4 us
    dot_general x10, matrix products, mul(): return jnp.einsum(spec, left, right, preferred_element_type=F32)  19.7 us
    all_to_all x1, blocking collectives, on_device(): lax.all_to_all(rows.reshape(pairs, NT // pairs, points, 2, NC), 'pair', s...  13.5 us
  transfers between devices with their start and end apart: 4, of which 4 were waited for; matrix products, arithmetic and copies ran while one was open for 5% of the time, Pallas kernels for 0%

commit v1 on v0

--- a/solution.py
+++ b/solution.py
@@ -24,7 +24,9 @@
     blocks = slab_cols // GBLK
     pairs = lax.axis_size("pair")
     slabs = lax.axis_size("ga")
-    whole_con = lax.all_gather(con_density, "ga", axis=0, tiled=True)
+    whole_con = jnp.concatenate(
+        lax.all_to_all(jnp.stack([con_density] * lax.axis_size("ga")), "ga", 0, 0), axis=0
+    )
     whole_val = lax.all_gather(val_density, "pair", axis=0, tiled=True)
     whole_here = lax.all_gather(trans_here, "pair", axis=0, tiled=True)
     within = (shift_map % GBLK).reshape(points, blocks, GBLK)

time: 405 us -> 388 us (0.958)
  waiting for transfers between devices: 285 us -> 236 us
  local copies, waits for them, and re-layouts: 39.7 us -> 51.6 us
  matrix products: 21.6 us -> 31 us
  starting transfers between devices: 0.12 us -> 9.07 us
    all_gather x1 -> x0, waiting for transfers between devices: 66.7 us -> none  [on_device(): whole_con = lax.all_gather(con_density, 'ga', axis=0, tiled=True)]
    all_gather x1, waiting for transfers between devices: 62.1 us -> 75.5 us  [on_device(): whole_val = lax.all_gather(val_density, 'pair', axis=0, tiled=True)]
    dot_general x10, matrix products: 19.7 us -> 29 us  [mul(): return jnp.einsum(spec, left, right, preferred_element_type=F32)]
    all_to_all x0 -> x1, starting transfers between devices: none -> 8.77 us  [on_device(): lax.all_to_all(jnp.stack([con_density] * lax.axis_size('ga')), 'ga', 0, 0)]
    reshape x4, local copies, waits for them, and re-layouts: 4.09 us -> 9.29 us  [unshift(): return moved.reshape(points, NV * NV, slab_cols)]
    reduce_scatter x1, waiting for transfers between devices: 70.6 us -> 75.1 us  [on_device(): lax.psum_scatter(direct, 'pair', scatter_dimension=0, tiled=True)[0]]
    unnamed x37 -> x34, local copies, waits for them, and re-layouts: 5.97 us -> 8.96 us
  transfers between devices with their start and end apart: 4 -> 4, of which waited for: 4 -> 3; matrix products, arithmetic and copies ran while one was open for 5% -> 9% of each run, Pallas kernels for 0% -> 0%
where the time goes in v1:
time: 388 us; the launch traced here: 387 us
  waiting for transfers between devices  236 us (61%)
  local copies, waits for them, and re-layouts  51.6 us (13%)
  blocking collectives  40.1 us (10%)
  matrix products  31 us (8%)
  between operations  13.4 us (3%)
  starting transfers between devices  9.07 us (2%)
  other arithmetic  5.81 us (1%)
    reduce_scatter x1, waiting for transfers between devices, on_device(): cols = lax.psum_scatter(cols, 'ga', scatter_dimension=0, tiled=True)  85.4 us
    all_gather x1, waiting for transfers between devices, on_device(): whole_val = lax.all_gather(val_density, 'pair', axis=0, tiled=True)  75.5 us
    reduce_scatter x1, waiting for transfers between devices, on_device(): lax.psum_scatter(direct, 'pair', scatter_dimension=0, tiled=True)[0]  75.1 us
    dot_general x10, matrix products, mul(): return jnp.einsum(spec, left, right, preferred_element_type=F32)  29 us
    all_gather x1, blocking collectives, on_device(): whole_here = lax.all_gather(trans_here, 'pair', axis=0, tiled=True)  26.6 us
    all_to_all x1, blocking collectives, on_device(): lax.all_to_all(rows.reshape(pairs, NT // pairs, points, 2, NC), 'pair', s...  13.5 us
    reshape x4, local copies, waits for them, and re-layouts, unshift(): return moved.reshape(points, NV * NV, slab_cols)  9.29 us
    unnamed x34, local copies, waits for them, and re-layouts  8.96 us
  transfers between devices with their start and end apart: 4, of which 3 were waited for; matrix products, arithmetic and copies ran while one was open for 9% of the time, Pallas kernels for 0%

profile of v1, /device:TPU:2, one launch (start us, length us, event | category | flops | bytes accessed | tf_op | source)
XLA Modules:
  0.0 387.1 jit_solution(17503753351443991228)
XLA Ops:
  6.5 1.1 copy.95
  7.6 3.6 stack.17
  11.2 8.8 %all-to-all-start = ((bf16[16,36,3,2,512]{4,3,1,2,0:T(2,128)(2,1)}), bf16[16,36,3,2,512]{4,3,1,2,0:T(2,128)(2,1)S(1)}, u32[]{:S(2)}, u32[]{:S(2)}) async-start(bf16[16,36,3,2,512]{4,3,1,2,0:T(2,128)(2,1)} %stack.17), calls=%async_computation | async-start | bytes 7077888 | tf_op jit(solution)/shard_map/all_to_all | solution.py:28
  20.0 1.6 copy.84
  21.9 75.5 %all-gather.2.cloned.1.call-done = bf16[256,3,2,512]{3,0,1,2:T(8,128)(2,1)} async-done(((bf16[16,3,2,512]{3,0,1,2:T(8,128)(2,1)}), bf16[256,3,2,512]{3,0,1,2:T(8,128)(2,1)}) %all-gather.2.cloned.1.call-update) | async-done | bytes 1572880 | tf_op jit(solution)/shard_map/all_gather | solution.py:30
  97.4 2.4 fusion.22
  100.0 2.7 fusion.42
  102.7 1.3 convolution_convert_fusion.1
  103.9 2.3 copy.94
  106.2 2.4 fusion.20
  108.8 2.6 fusion.43
  111.5 1.3 convolution_convert_fusion
  112.7 2.4 copy.92
  115.1 2.4 convolution_convert_fusion.3
  117.5 2.3 copy.93
  119.8 2.4 convolution_convert_fusion.2
  122.2 2.3 copy.89
  124.5 2.1 neg.7
  126.7 2.2 neg.6
  128.8 2.4 copy.96
  131.3 4.2 %copy.97 = bf16[3,576,2,512]{3,2,1,0:T(2,128)(2,1)} copy(bf16[3,576,2,512]{3,2,0,1:T(2,128)(2,1)S(1)} %bitcast.117) | data formatting | bytes 7077888 | tf_op jit(solution)/shard_map/transpose | solution.py:56
  135.4 7.8 %reshape.60 = bf16[3,576,1024]{2,1,0:T(8,128)(2,1)S(1)} reshape(bf16[3,576,2,512]{3,2,1,0:T(2,128)(2,1)} %copy.97) | data formatting | bytes 7077888 | tf_op jit(solution)/shard_map/reshape | solution.py:56
  143.3 0.5 constant_dynamic-update-slice_fusion.1
  143.8 0.5 constant_dynamic-update-slice_fusion
  144.3 2.9 copy-done.4
  147.2 6.3 %fusion.8 = f32[3,256,576]{2,1,0:T(8,128)S(1)} fusion(bf16[3,576,2048]{2,1,0:T(8,128)(2,1)S(1)} %constant_dynamic-update-slice_fusion, bf16[3,256,512]{2,1,0:T(8,128)(2,1)} %copy.94, bf16[3,256,512]{2,1,0:T(8,128)(2,1)S(1)} %copy-done.2, bf16[3,256,512]{2,1,0:T(8,128)(2,1)} %copy.93, bf16[3,256,512]{2,1,0:T(8,128)(2,1)S(1)} %copy-done.3), kind=kOutput, calls=%fused_computation.11 | convolution fusion | flops 1824522240 | bytes 11993088 | tf_op jit(solution)/shard_map/kax,kbx->kab/dot_general | solution.py:38
  153.6 5.4 %fusion = f32[3,256,576]{2,1,0:T(8,128)S(1)} fusion(bf16[3,576,2048]{2,1,0:T(8,128)(2,1)} %copy-done.4, bf16[3,256,512]{2,1,0:T(8,128)(2,1)S(1)} %copy-done.7, bf16[3,256,512]{2,1,0:T(8,128)(2,1)S(1)} %copy-done.5, bf16[3,256,512]{2,1,0:T(8,128)(2,1)S(1)} %copy-done.8, bf16[3,256,512]{2,1,0:T(8,128)(2,1)S(1)} %copy-done.6), kind=kOutput, calls=%fused_computation.3 | convolution fusion | flops 1824522240 | bytes 11993088 | tf_op jit(solution)/shard_map/kax,kbx->kab/dot_general | solution.py:38
  159.3 3.1 copy.104
  162.4 0.7 copy-done.10
  163.3 26.6 %all_gather.6 = bf16[384,2,512]{2,0,1:T(8,128)(2,1)S(1)} all-gather(bf16[24,2,512]{2,0,1:T(8,128)(2,1)S(1)} %copy.83), channel_id=1, replica_groups=mesh['ga'=16,'pair'=16] {'pair'}, dimensions={0}, use_global_device_ids=true | all-gather | bytes 835584 | tf_op jit(solution)/shard_map/all_gather | solution.py:31
  190.0 0.5 fusion.56
  190.4 0.5 fusion.38
  190.9 0.5 fusion.57
  191.4 0.5 fusion.39
  191.9 75.1 %reduce-scatter.3.cloned.1.call-done = f32[1,3,2,16,576]{4,3,2,1,0:T(8,128)} async-done(((f32[16,3,2,16,576]{4,3,2,1,0:T(8,128)}), f32[1,3,2,16,576]{4,3,2,1,0:T(8,128)}) %reduce-scatter.3.cloned.1.call-update) | async-done | bytes 221200 | tf_op jit(solution)/shard_map/reduce_scatter | solution.py:62
  267.0 1.4 reshape_squeeze.3
  268.8 0.8 copy.106
  269.6 3.3 gather_fusion
  273.1 0.9 reshape.86
  274.0 13.5 %all_to_all.10 = f32[16,1,3456]{2,1,0:T(1,128)S(1)} all-to-all(f32[16,1,3456]{2,1,0:T(1,128)S(1)} %reshape.86), channel_id=1, replica_groups=mesh['ga'=16,'pair'=16] {'pair'}, dimensions={0} | all-to-all | bytes 442368 | tf_op jit(solution)/shard_map/all_to_all | solution.py:77
  287.4 0.5 broadcast.27
  288.0 1.2 reduce
  289.1 0.7 reshape.87
  289.9 0.8 copy.114
  290.8 0.7 reshape.85
  291.5 2.2 gather_fusion.1
  293.7 85.4 %reduce-scatter.5.cloned.1.call-done = f32[24,144]{1,0:T(8,128)} async-done(((f32[384,144]{1,0:T(8,128)}), f32[24,144]{1,0:T(8,128)}) %reduce-scatter.5.cloned.1.call-update) | async-done | bytes 13840 | tf_op jit(solution)/shard_map/reduce_scatter | solution.py:82
  379.1 1.5 copy.115
  (44 shorter events, 1.8 us)
Async XLA Ops:
  11.2 10.6 %copy-start.12 = (s32[3,512]{1,0:T(4,128)S(1)}, s32[3,512]{1,0:T(4,128)}, u32[]{:S(2)}) copy-start(s32[3,512]{1,0:T(4,128)} %param.14) | copy-start | bytes 18436
  11.2 117.6 %all-to-all-start = ((bf16[16,36,3,2,512]{4,3,1,2,0:T(2,128)(2,1)}), bf16[16,36,3,2,512]{4,3,1,2,0:T(2,128)(2,1)S(1)}, u32[]{:S(2)}, u32[]{:S(2)}) async-start(bf16[16,36,3,2,512]{4,3,1,2,0:T(2,128)(2,1)} %stack.17), calls=%async_computation | async-start | bytes 7077888 | tf_op jit(solution)/shard_map/all_to_all | solution.py:28
  20.0 77.4 %all-gather.2.cloned.1.call-start = ((), (), s32[]{:S(2)}) async-start(), calls=%async_computation.4 | async-start | bytes 1671168 | tf_op jit(solution)/shard_map/all_gather | solution.py:30
  21.6 245.4 %reduce-scatter.3.cloned.1.call-start = ((), (), s32[]{:S(2)}) async-start(), calls=%async_computation.5 | async-start | bytes 4177920 | tf_op jit(solution)/shard_map/reduce_scatter | solution.py:62
  97.4 2.6 copy-start
  106.2 2.6 copy-start.1
  143.8 3.4 copy-start.2
  143.8 3.4 copy-start.3
  144.3 2.9 copy-start.4
  147.2 6.4 %copy-start.5 = (bf16[3,256,512]{2,1,0:T(8,128)(2,1)S(1)}, bf16[3,256,512]{2,1,0:T(8,128)(2,1)}, u32[]{:S(2)}) copy-start(bf16[3,256,512]{2,1,0:T(8,128)(2,1)} %copy.94) | copy-start | bytes 2359300
  147.2 6.4 %copy-start.6 = (bf16[3,256,512]{2,1,0:T(8,128)(2,1)S(1)}, bf16[3,256,512]{2,1,0:T(8,128)(2,1)}, u32[]{:S(2)}) copy-start(bf16[3,256,512]{2,1,0:T(8,128)(2,1)} %copy.93) | copy-start | bytes 2359300
  147.2 6.4 %copy-start.7 = (bf16[3,256,512]{2,1,0:T(8,128)(2,1)S(1)}, bf16[3,256,512]{2,1,0:T(8,128)(2,1)}, u32[]{:S(2)}) copy-start(bf16[3,256,512]{2,1,0:T(8,128)(2,1)} %neg.7) | copy-start | bytes 2359300
  147.2 6.4 %copy-start.8 = (bf16[3,256,512]{2,1,0:T(8,128)(2,1)S(1)}, bf16[3,256,512]{2,1,0:T(8,128)(2,1)}, u32[]{:S(2)}) copy-start(bf16[3,256,512]{2,1,0:T(8,128)(2,1)} %neg.6) | copy-start | bytes 2359300
  162.3 0.8 copy-start.10
  162.3 0.8 copy-start.13
  162.3 1.0 copy-start.9
  162.3 1.0 copy-start.11
  162.4 216.8 %reduce-scatter.5.cloned.1.call-start = ((), (), s32[]{:S(2)}) async-start(), calls=%async_computation.6 | async-start | bytes 417792 | tf_op jit(solution)/shard_map/reduce_scatter | solution.py:82
Sparse Core Ops, SparseCore 0:
  23.6 73.7 all-gather.1
  162.5 104.4 reduce-scatter.2
  293.8 85.2 reduce-scatter.4
